TPU v7x, 256 devices: a whole 4x4x8 slice. The times are simulated.
256 devices in a mesh: row: 8 (over y_lo, x), col: 32 (over z, y_hi, core).
Axes of the slice: x: 4, y: 4 (y_hi: 2, y_lo: 2; y = y_hi * 2 + y_lo), z: 8, core: 2. Of those that a mesh axis runs over, the one named last changes fastest.
Arguments:
- descriptors: bfloat16 [24576, 768], P(('row', 'col')), may hold values from -6 to 6
- coefficients: bfloat16 [24576, 256], P('col'), may hold values from -0.119628906 to 0.119628906
- targets: float32 [24576, 256], P(('row', 'col')), may hold values from -6 to 6
- whitening: float32 [2, 256, 256], replicated, may hold values from -1 to 2, as said below
Outputs:
- updated: float32 [24576, 24576], P('row', 'col')
- residual: float32 [24576, 256], P(('row', 'col'))
Inputs may be any that keep to these rules, and one draw needn't show every extreme that they name: whitening holds two given 256 x 256 matrices; nothing more is assumed of them.
All inputs are finite; a program needn't handle non-finite values.
Results may differ from a plain program's by a relative error of at most 0.0029.
Values may be sent and summed in bfloat16 or wider, within the bound.
A program may use at most 128 MiB of HBM per device.

v0:
```python
import jax
import jax.numpy as jnp
from jax import lax
from jax.sharding import PartitionSpec as P

F = 768


RIDGE = 0.5


def broadcast(block, axis, holder):
    block = jnp.where(lax.axis_index(axis) == holder, block, jnp.zeros_like(block))
    return lax.psum(block, axis)


def kernel_block(left_points, right_points, left_first, right_first):
    inner = lax.dot_general(
        left_points, right_points, (((1,), (1,)), ((), ())), preferred_element_type=jnp.float32
    )
    left_sq = jnp.sum(jnp.square(left_points.astype(jnp.float32)), axis=1)
    right_sq = jnp.sum(jnp.square(right_points.astype(jnp.float32)), axis=1)
    distance = left_sq[:, None] + right_sq[None, :] - 2.0 * inner
    values = jnp.exp(-distance / (2.0 * F))
    left_ids = left_first + jnp.arange(left_points.shape[0], dtype=jnp.int32)
    right_ids = right_first + jnp.arange(right_points.shape[0], dtype=jnp.int32)
    return values + jnp.where(left_ids[:, None] == right_ids[None, :], RIDGE, 0.0)


def outer_rows(left_panel, right_panel):
    return lax.dot_general(
        left_panel, right_panel, (((1,), (1,)), ((), ())), preferred_element_type=jnp.float32
    )


def whiten(values, matrix):
    return jnp.dot(
        values, matrix, precision=lax.Precision.HIGHEST, preferred_element_type=jnp.float32
    ).astype(jnp.bfloat16)


def body(descriptors, coefficients, targets, whitening):
    row_count = lax.axis_size("row")
    col_count = lax.axis_size("col")
    per_block = col_count // row_count
    row_index = lax.axis_index("row")
    col_index = lax.axis_index("col")
    cols_dev = coefficients.shape[0]
    shard_rows = targets.shape[0]
    panel_width = whitening.shape[1]
    row_points = lax.all_gather(descriptors, "col", axis=0, tiled=True)
    rows_dev = row_points.shape[0]
    piece_start = col_index % per_block * cols_dev
    own_piece = lax.dynamic_slice_in_dim(row_points, piece_start, cols_dev, 0)
    col_points = broadcast(own_piece, "row", col_index // per_block)
    row_first = row_index * rows_dev
    col_first = col_index * cols_dev
    kernel_tile = kernel_block(row_points, col_points, row_first, col_first)
    kernel_copy = kernel_tile.astype(jnp.bfloat16)
    partial_term = jnp.dot(kernel_copy, coefficients, preferred_element_type=jnp.float32)
    summed = lax.psum(partial_term, "col")
    own_rows = lax.dynamic_slice_in_dim(summed, col_index * shard_rows, shard_rows, 0)
    residual = targets - own_rows
    current = kernel_tile
    for which in range(2):
        owner_col = which * panel_width // cols_dev
        offset = which * panel_width % cols_dev
        matrix = whitening[which]
        source = current

        def make_panel():
            return whiten(source[:, offset : offset + panel_width], matrix)

        def empty_panel():
            return jnp.zeros((rows_dev, panel_width), jnp.bfloat16)

        panel_here = lax.cond(col_index == owner_col, make_panel, empty_panel)
        panel_rows = broadcast(panel_here, "col", owner_col)
        panel_piece = lax.dynamic_slice_in_dim(panel_rows, piece_start, cols_dev, 0)
        panel_cols = broadcast(panel_piece, "row", col_index // per_block)
        current = current - outer_rows(panel_rows, panel_cols)
    return (current, residual)


def solution(mesh):
    in_specs = (P(("row", "col"), None), P("col", None), P(("row", "col"), None), P())
    out_specs = (P("row", "col"), P(("row", "col"), None))
    return jax.shard_map(body, mesh=mesh, in_specs=in_specs, out_specs=out_specs, check_vma=False)
```

profile of v0, /device:TPU:70, one launch (start us, length us, event | category | flops | bytes accessed | tf_op | source)
XLA Modules:
  0.0 1239.3 jit_solution(14336629977801103511)
XLA Ops:
  7.2 0.0 copy-start
  7.2 0.0 all-gather.2.cloned.1.call-start
  7.2 0.7 all-gather.2.cloned.1.call-update
  7.9 0.0 all-reduce.7.cloned.1.call-start
  8.0 92.0 %all-gather.2.cloned.1.call-done = bf16[3072,768]{1,0:T(8,128)(2,1)} async-done(((bf16[96,768]{1,0:T(8,128)(2,1)}), bf16[3072,768]{1,0:T(8,128)(2,1)}) %all-gather.2.cloned.1.call-update) | async-done | bytes 4718608 | tf_op jit(solution)/shard_map/all_gather | solution.py:51
  100.0 2.5 dynamic-slice_select_fusion
  102.5 0.0 all-reduce.7.cloned.1.call-update
  102.5 0.0 all-reduce.9.cloned.1.call-start
  102.6 3.3 multiply_reduce_fusion
  105.9 76.4 %all-reduce.7.cloned.1.call-done = bf16[768,768]{1,0:T(8,128)(2,1)} async-done(((bf16[768,768]{1,0:T(8,128)(2,1)}), bf16[768,768]{1,0:T(8,128)(2,1)}) %all-reduce.7.cloned.1.call-update) | async-done | bytes 1179664 | tf_op jit(solution)/shard_map/psum | solution.py:14
  182.3 1.6 multiply_reduce_fusion.1
  183.9 0.0 copy-start.1
  183.9 11.3 fusion.9
  195.2 0.0 copy-done.1
  195.2 0.1 conditional.2
  195.2 0.1 broadcast.23
  195.3 1.3 broadcast_select_fusion.1
  196.6 0.0 all-reduce.9.cloned.1.call-update
  196.6 0.0 all-reduce.11.cloned.1.call-start
  196.7 273.1 %all-reduce.9.cloned.1.call-done = bf16[3072,256]{1,0:T(8,128)(2,1)} async-done(((bf16[3072,256]{1,0:T(8,128)(2,1)}), bf16[3072,256]{1,0:T(8,128)(2,1)}) %all-reduce.9.cloned.1.call-update) | async-done | bytes 1572880 | tf_op jit(solution)/shard_map/psum | solution.py:14
  469.7 1.8 dynamic-slice_select_fusion.2
  471.5 0.0 all-reduce.11.cloned.1.call-update
  471.6 0.0 all-reduce.13.cloned.1.call-start
  471.6 87.3 %all-reduce.11.cloned.1.call-done = bf16[768,256]{1,0:T(8,128)(2,1)} async-done(((bf16[768,256]{1,0:T(8,128)(2,1)}), bf16[768,256]{1,0:T(8,128)(2,1)}) %all-reduce.11.cloned.1.call-update) | async-done | bytes 393232 | tf_op jit(solution)/shard_map/psum | solution.py:14
  558.9 9.3 convolution_subtract_fusion.1
  568.2 0.3 conditional.3
  568.2 0.1 broadcast.24
  568.5 1.3 broadcast_select_fusion
  569.8 0.0 all-reduce.13.cloned.1.call-update
  569.8 0.0 all-reduce.17.cloned.1.call-start
  569.9 0.0 copy-done
  569.9 6.8 fusion.10
  576.6 0.0 copy-start.2
  576.6 0.0 all-reduce.17.cloned.1.call-update
  576.7 0.0 all-reduce.15.cloned.1.call-start
  576.7 266.3 %all-reduce.13.cloned.1.call-done = bf16[3072,256]{1,0:T(8,128)(2,1)} async-done(((bf16[3072,256]{1,0:T(8,128)(2,1)}), bf16[3072,256]{1,0:T(8,128)(2,1)}) %all-reduce.13.cloned.1.call-update) | async-done | bytes 1572880 | tf_op jit(solution)/shard_map/psum | solution.py:14
  843.0 1.8 dynamic-slice_select_fusion.1
  844.8 0.0 all-reduce.15.cloned.1.call-update
  844.8 278.1 %all-reduce.17.cloned.1.call-done = f32[3072,256]{1,0:T(8,128)} async-done(((f32[3072,256]{1,0:T(8,128)}), f32[3072,256]{1,0:T(8,128)}) %all-reduce.17.cloned.1.call-update) | async-done | bytes 3145744 | tf_op jit(solution)/shard_map/psum | solution.py:61
  1122.9 0.0 copy-done.2
  1122.9 1.5 dynamic-slice_subtract_fusion
  1124.5 89.0 %all-reduce.15.cloned.1.call-done = bf16[768,256]{1,0:T(8,128)(2,1)} async-done(((bf16[768,256]{1,0:T(8,128)(2,1)}), bf16[768,256]{1,0:T(8,128)(2,1)}) %all-reduce.15.cloned.1.call-update) | async-done | bytes 393232 | tf_op jit(solution)/shard_map/psum | solution.py:14
  1213.5 9.3 convolution_subtract_fusion
  1222.8 9.6 copy.10
  (2 shorter events, 0.0 us)
Async XLA Ops:
  7.2 562.7 %copy-start = (bf16[768,256]{1,0:T(8,128)(2,1)S(1)}, bf16[768,256]{1,0:T(8,128)(2,1)}, u32[]{:S(2)}) copy-start(bf16[768,256]{1,0:T(8,128)(2,1)} %param.9) | copy-start | bytes 1179652
  7.2 92.8 %all-gather.2.cloned.1.call-start = ((), (), s32[]{:S(2)}) async-start(), calls=%async_computation | async-start | bytes 4866048 | tf_op jit(solution)/shard_map/all_gather | solution.py:51
  7.9 174.4 %all-reduce.7.cloned.1.call-start = ((), (), s32[]{:S(2)}) async-start(), calls=%async_computation.1 | async-start | bytes 2359296 | tf_op jit(solution)/shard_map/psum | solution.py:14
  102.5 367.2 %all-reduce.9.cloned.1.call-start = ((), (), s32[]{:S(2)}) async-start(), calls=%async_computation.2 | async-start | bytes 3145728 | tf_op jit(solution)/shard_map/psum | solution.py:14
  183.9 11.3 copy-start.1
  196.6 362.3 %all-reduce.11.cloned.1.call-start = ((), (), s32[]{:S(2)}) async-start(), calls=%async_computation.3 | async-start | bytes 786432 | tf_op jit(solution)/shard_map/psum | solution.py:14
  471.6 371.5 %all-reduce.13.cloned.1.call-start = ((), (), s32[]{:S(2)}) async-start(), calls=%async_computation.4 | async-start | bytes 3145728 | tf_op jit(solution)/shard_map/psum | solution.py:14
  569.8 553.1 %all-reduce.17.cloned.1.call-start = ((), (), s32[]{:S(2)}) async-start(), calls=%async_computation.6 | async-start | bytes 6291456 | tf_op jit(solution)/shard_map/psum | solution.py:61
  576.6 546.3 %copy-start.2 = (f32[96,256]{1,0:T(8,128)S(1)}, f32[96,256]{1,0:T(8,128)}, u32[]{:S(2)}) copy-start(f32[96,256]{1,0:T(8,128)} %param.10) | copy-start | bytes 294916
  576.7 636.8 %all-reduce.15.cloned.1.call-start = ((), (), s32[]{:S(2)}) async-start(), calls=%async_computation.5 | async-start | bytes 786432 | tf_op jit(solution)/shard_map/psum | solution.py:14
Sparse Core Ops, SparseCore 0:
  10.8 89.2 all-gather.1
  103.2 79.0 all-reduce.6
  196.7 272.9 all-reduce.8
  472.2 86.6 all-reduce.10
  569.9 273.0 all-reduce.12
  845.5 277.3 all-reduce.16
  1126.1 87.3 all-reduce.14
where the time goes:
time: 1240 us
  waiting for transfers between devices  1160 us (94%)
  matrix products  36.7 us (3%)
  other arithmetic  15.1 us (1%)
  between operations  14.2 us (1%)
    psum x5, waiting for transfers between devices, broadcast(): return lax.psum(block, axis)  792 us
    psum x1, waiting for transfers between devices, body(): summed = lax.psum(partial_term, 'col')  278 us
    all_gather x1, waiting for transfers between devices, body(): row_points = lax.all_gather(descriptors, 'col', axis=0, tiled=True)  92 us
  transfers between devices with their start and end apart: 7, of which 7 were waited for; matrix products, arithmetic and copies ran while one was open for 1% of the time, Pallas kernels for 0%

commit v1 on v0

v1 whole, which is shorter than its diff:
```python
import functools
import jax
import jax.numpy as jnp
from jax import lax
from jax.experimental import pallas as pl
from jax.experimental.pallas import tpu as pltpu
from jax.sharding import PartitionSpec as P

MESH = pl.DeviceIdType.MESH
SHARD, F = 96, 768
ROWS, COLS = 3072, 768
STOP = "m"


def place():
    r = lax.axis_index("row")
    c = lax.axis_index("col")
    return r % 4, r // 4, (c // 2) % 2, c // 4, c % 2


def device(x, l, h, z, k):
    return (l * 4 + x, z * 4 + h * 2 + k)


class Sender:
    def __init__(self, sems):
        self.sems = sems
        self.items = []

    def send(self, src, dst, recv, dev, cond=None):
        n = len(self.items)

        def make():
            return pltpu.make_async_remote_copy(
                src, dst, self.sems.at[n], recv, device_id=dev, device_id_type=MESH
            )

        self.items.append((make, cond))
        if cond is None:
            make().start()
        else:
            pl.when(cond)(lambda: make().start())

    def drain(self):
        for make, cond in self.items:
            if cond is None:
                make().wait_send()
            else:
                pl.when(cond)(lambda make=make: make().wait_send())


def gather_kernel(x_in, xr, xc, xp, ssem, za, zb, yb, yc, sa, sb, sc, xps, xms, yx, op, om, op2, om2, p1, p2, p3, loc):
    x, l, h, z, k = place()
    r = l * 4 + x
    c = z * 4 + h * 2 + k
    zplus, zminus = device(x, l, h, (z + 1) % 8, k), device(x, l, h, (z + 7) % 8, k)
    ypart, sib = device(x, l, 1 - h, z, k), device(x, l, h, z, 1 - k)
    xplus, xminus = device((x + 1) % 4, l, h, z, k), device((x + 3) % 4, l, h, z, k)
    yl = device(x, 1 - l, h, z, k)

    def arrived(ref, sem, cond=None):
        def wait():
            pltpu.make_async_copy(ref, ref, sem).wait()

        if cond is None:
            wait()
        else:
            pl.when(cond)(wait)

    t = 4 * r + 2 * h + k
    owner = t // 6
    is_owner = jnp.logical_and(r == 0, c < 6)
    self_piece = jnp.logical_and(r == 0, c == 0)
    bar = pltpu.get_barrier_semaphore()

    def hello(dev):
        pl.semaphore_signal(bar, inc=1, device_id=dev, device_id_type=MESH)

    for dev in (zplus, zminus, sib):
        hello(dev)
    for i in range(1, 16):
        rr = (r + i // 2) % 8
        hh = (h + i) % 2
        hello((rr, z * 4 + hh * 2 + k))
    pl.when(jnp.logical_not(self_piece))(lambda: hello((0, owner)))
    extra = jnp.where(c == 0, 47, jnp.where(c < 5, 48, 16))
    pl.semaphore_wait(bar, 18 + jnp.where(is_owner, extra, 0))

    out = Sender(ssem)

    def rows(start, n):
        return xr.at[pl.ds(pl.multiple_of(start, 16), n)]

    def first(p, hh, kk):
        return 384 * p + 96 * (2 * hh + kk)

    own = first(z, h, k)
    own_copy = pltpu.make_async_copy(x_in, rows(own, 96), loc.at[0])
    own_copy.start()
    out.send(x_in.at[pl.ds(0, 48)], rows(own, 48), yb.at[0], ypart)
    out.send(x_in, rows(own, 96), za.at[0], zplus)
    out.send(x_in, rows(own, 96), za.at[1], zminus)
    out.send(x_in.at[pl.ds(48, 48)], rows(own + 48, 48), yc.at[0], ypart)
    out.send(x_in, rows(own, 96), sa.at[0], sib)
    for j in range(0 if 'p' in STOP else 6):
        tt = 6 * c + j
        piece = jnp.logical_and(is_owner, tt < 32)
        for zz in range(8):
            here = jnp.logical_and(piece, jnp.logical_or(tt > 0, z != zz)) if (j == 0 and zz == 0) else piece
            out.send(
                x_in.at[pl.ds(16 * j, 16)],
                xp.at[tt // 4, (tt // 2) % 2, tt % 2],
                p1.at[0],
                (tt // 4, zz * 4 + tt % 4),
                here,
            )

    def mine():
        copy = pltpu.make_async_copy(x_in.at[pl.ds(0, 16)], xp.at[0, 0, 0], loc.at[1])
        copy.start()
        copy.wait()

    pl.when(self_piece)(mine)

    def plane(s, d):
        return (z + 16 - d * s) % 8

    arrived(rows(first(z, 1 - h, k), 48), yb.at[0])
    part = rows(first(z, 1 - h, k), 48)
    out.send(part, part, zb.at[0], zplus)
    out.send(part, part, zb.at[1], zminus)
    out.send(part, part, sb.at[0], sib)

    def late(s):
        for n, d in enumerate((1, -1)):
            if s in (0, 4) and n == 1:
                continue
            i = 0 if s == 0 else (2 * s - 1 + n)
            p = plane(s, d)
            piece = rows(first(p, 1 - h, k) + 48, 48)
            arrived(piece, yc.at[i])
            out.send(piece, piece, sc.at[i], sib)
        for n, d in enumerate((1, -1)):
            if s in (0, 4) and n == 1:
                continue
            i = 0 if s == 0 else (2 * s - 1 + n)
            p = plane(s, d)
            arrived(rows(first(p, h, 1 - k), 96), sa.at[i])
            arrived(rows(first(p, 1 - h, 1 - k), 48), sb.at[i])
            arrived(rows(first(p, 1 - h, 1 - k) + 48, 48), sc.at[i])

    for s in range(1, 5):
        if s < 4:
            for n, d in enumerate((1, -1)):
                i = 2 * s - 1 + n
                p = plane(s, d)
                a = rows(first(p, h, k), 96)
                arrived(a, za.at[i - 1])
                if s < 3:
                    out.send(a, a, za.at[i + 1], zplus if d == 1 else zminus)
                c_half = rows(first(p, h, k) + 48, 48)
                out.send(c_half, c_half, yc.at[i], ypart)
                out.send(a, a, sa.at[i], sib)
            if s == 3:
                da = 1 - 2 * k
                a = rows(first((z + 16 - 3 * da) % 8, h, k), 96)
                out.send(a, a, za.at[6], device(x, l, h, (z + 8 + da) % 8, k))
            for n, d in enumerate((1, -1)):
                i = 2 * s - 1 + n
                p = plane(s, d)
                b = rows(first(p, 1 - h, k), 48)
                arrived(b, zb.at[i - 1])
                if s < 3:
                    out.send(b, b, zb.at[i + 1], zplus if d == 1 else zminus)
                out.send(b, b, sb.at[i], sib)
            if s == 3:
                b = rows(first((z + 16 + 3 * da) % 8, 1 - h, k), 48)
                out.send(b, b, zb.at[6], device(x, l, h, (z + 8 - da) % 8, k))
        else:
            p = plane(4, 1)
            a = rows(first(p, h, k), 96)
            arrived(a, za.at[6])
            c_half = rows(first(p, h, k) + 48, 48)
            out.send(c_half, c_half, yc.at[7], ypart)
            out.send(a, a, sa.at[7], sib)
            b = rows(first(p, 1 - h, k), 48)
            arrived(b, zb.at[6])
            out.send(b, b, sb.at[7], sib)
        if 'l' in STOP:
            pass
        elif 'm' in STOP:
            if s >= 2: late(s - 2)
        else:
            late(s - 1)
        if s == 1 and 'p' not in STOP:
            piece = xp.at[r, h, k]
            arrived(piece, p1.at[0], jnp.logical_not(self_piece))
            for i in range(1, 16):
                rr = (r + i // 2) % 8
                hh = (h + i) % 2
                out.send(piece, piece, p2.at[i - 1], (rr, z * 4 + hh * 2 + k))
        if s == 3 and 'p' not in STOP:
            for i in range(1, 16):
                rr = (r + 8 - i // 2) % 8
                hh = (h + i) % 2
                arrived(xp.at[rr, hh, k], p2.at[i - 1])
            mine_all = xp.at[:, :, k]
            out.send(mine_all, mine_all, p3.at[0], sib)
    own_copy.wait()
    for q in (range(5) if 'l' in STOP else (3, 4) if 'm' in STOP else (4,)): late(q)

    if 'c' in STOP:
        out.drain()
        return
    xs, ls = z % 4, z // 4
    q = (x + 4 - xs) % 4
    line = l == ls
    source = jnp.logical_and(line, q == 0)
    for_me = rows(768 * (2 * h + k), 768)
    keep = pltpu.make_async_copy(for_me, xc, loc.at[2])
    pl.when(source)(lambda: keep.start())
    pl.when(source)(lambda: keep.wait())

    def block(start, n):
        return xc.at[pl.ds(pl.multiple_of(start, 16), n)]

    def inside(i):
        return jnp.logical_and(line, jnp.logical_and(i >= 0, i < 8))

    qm = (4 - q) % 4
    for tau in range(11):
        i = tau - q
        u = (i + 4) % 4
        ok = inside(i)
        ic = jnp.clip(i, 0, 7)
        j = ic // 4
        piece = block(384 * j + 48 * u, 48)
        arrived(piece, xps.at[ic], jnp.logical_and(ok, q != 0))
        out.send(piece, piece, xps.at[ic], xplus, jnp.logical_and(ok, q != 3))
        out.send(piece, piece, yx.at[2 * j + u % 2], yl, jnp.logical_and(ok, q == jnp.where(u < 2, 1, 2)))
        i = tau - qm
        u = (i + 4) % 4
        ok = inside(i)
        ic = jnp.clip(i, 0, 7)
        j = ic // 4
        piece = block(384 * j + 192 + 48 * u, 48)
        arrived(piece, xms.at[ic], jnp.logical_and(ok, q != 0))
        out.send(piece, piece, xms.at[ic], xminus, jnp.logical_and(ok, q != 1))
        out.send(piece, piece, yx.at[2 * j + u % 2], yl, jnp.logical_and(ok, q == jnp.where(u < 2, 3, 0)))
    other = jnp.logical_not(line)
    b0 = (q + 3) % 4
    bm, bp = (q + 2) % 4, q
    for i in range(4):
        piece = block(384 * (i // 2) + 96 * b0 + 48 * (i % 2), 48)
        arrived(piece, yx.at[i], other)
        out.send(piece, piece, op.at[i], xplus, other)
        out.send(piece, piece, om.at[i], xminus, other)
    for j in range(2):
        for u in range(2):
            piece = block(384 * j + 96 * bm + 48 * u, 48)
            arrived(piece, op.at[2 * j + u], other)
            if u == 0:
                out.send(piece, piece, op2.at[j], xplus, other)
            piece = block(384 * j + 96 * bp + 48 * u, 48)
            arrived(piece, om.at[2 * j + u], other)
            if u == 1:
                out.send(piece, piece, om2.at[j], xminus, other)
    bo = (q + 1) % 4
    for j in range(2):
        arrived(block(384 * j + 96 * bo, 48), op2.at[j], other)
        arrived(block(384 * j + 96 * bo + 48, 48), om2.at[j], other)
    if 'p' not in STOP: arrived(xp.at[:, :, 1 - k], p3.at[0])
    out.drain()


def gather(descriptors):
    dma = pltpu.SemaphoreType.DMA
    vm = pl.BlockSpec(memory_space=pltpu.VMEM)
    return pl.pallas_call(
        gather_kernel,
        out_shape=(
            jax.ShapeDtypeStruct((ROWS, F), jnp.bfloat16),
            jax.ShapeDtypeStruct((COLS, F), jnp.bfloat16),
            jax.ShapeDtypeStruct((8, 2, 2, 16, F), jnp.bfloat16),
        ),
        in_specs=[vm],
        out_specs=(vm, vm, vm),
        scratch_shapes=[dma((240,)), dma((7,)), dma((7,)), dma((1,)), dma((8,)), dma((8,)), dma((8,)), dma((8,)),
                        dma((8,)), dma((8,)), dma((4,)), dma((4,)), dma((4,)), dma((2,)), dma((2,)),
                        dma((1,)), dma((15,)), dma((1,)), dma((3,))],
        compiler_params=pltpu.CompilerParams(collective_id=0, has_side_effects=True, vmem_limit_bytes=40 << 20),
        name="gather",
    )(descriptors)


RIDGE = 0.5
NRESP = 256
PANEL = 256
BLK = 384
BF, F32 = jnp.bfloat16, jnp.float32


def dot_t(a, b):
    return lax.dot_general(a, b, (((1,), (1,)), ((), ())), preferred_element_type=F32)


def dot(a, b):
    return jnp.dot(a, b, preferred_element_type=F32)


def halves(a):
    high = a.astype(BF)
    return high, (a - high.astype(F32)).astype(BF)


def whiten(values, w_high, w_low):
    high, low = halves(values)
    return (dot(high, w_high) + dot(high, w_low) + dot(low, w_high)).astype(BF)


def square_sums(points):
    wide = points.astype(F32)
    return jnp.sum(wide * wide, axis=1, keepdims=True)


def as_row(column):
    n = column.shape[0]
    return jnp.transpose(jnp.broadcast_to(column, (n, 128)))[0:1, :]


def gaussian(left, right, left_sums, right_sums):
    distance = left_sums + right_sums - 2.0 * dot_t(left, right)
    return jnp.exp(distance * (-1.0 / (2.0 * F)))


def with_ridge(values, gap):
    i = lax.broadcasted_iota(jnp.int32, values.shape, 0)
    j = lax.broadcasted_iota(jnp.int32, values.shape, 1)
    return values + jnp.where(i - j == gap, RIDGE, 0.0)


def tile_kernel(xr, xc, xp, coef, w, upd, part, top, pc, sp, sj, wh, wl):
    b = pl.program_id(0)
    row0 = lax.axis_index("row") * ROWS + b * BLK
    col0 = lax.axis_index("col") * COLS

    def panels(points, sums, first):
        k0 = with_ridge(gaussian(points, xp[...], sums, sp[...]), -first)
        p1 = whiten(k0[:, :PANEL], wh[0], wl[0])
        k1 = k0[:, PANEL:] - dot_t(p1, top[...])
        return p1, whiten(k1, wh[1], wl[1])

    @pl.when(b == 0)
    def _():
        for i in range(2):
            high, low = halves(w[i])
            wh[i] = high
            wl[i] = low
        sp[...] = as_row(square_sums(xp[...]))
        sj[...] = as_row(square_sums(xc[...]))
        lower = xp[PANEL:, :]
        k0 = gaussian(lower, xp[:PANEL, :], square_sums(lower), sp[:, :PANEL])
        top[...] = whiten(k0, wh[0], wl[0])
        for i in range(2):
            points = xc[pl.ds(BLK * i, BLK), :]
            p1, p2 = panels(points, square_sums(points), col0 + BLK * i)
            pc[pl.ds(BLK * i, BLK), :PANEL] = p1
            pc[pl.ds(BLK * i, BLK), PANEL:] = p2

    points = xr[...]
    sums = square_sums(points)
    kern = with_ridge(gaussian(points, xc[...], sums, sj[...]), col0 - row0)
    part[...] = dot(kern.astype(BF), coef[...])
    p1, p2 = panels(points, sums, row0)
    upd[...] = kern - dot_t(p1, pc[:, :PANEL]) - dot_t(p2, pc[:, PANEL:])


def tile(xr, xc, xp, coef, w):
    whole = lambda *shape: pl.BlockSpec(shape, lambda b: (0,) * len(shape))
    return pl.pallas_call(
        tile_kernel,
        grid=(ROWS // BLK,),
        out_shape=(jax.ShapeDtypeStruct((ROWS, COLS), F32), jax.ShapeDtypeStruct((ROWS, NRESP), F32)),
        in_specs=[pl.BlockSpec((BLK, F), lambda b: (b, 0)), whole(COLS, F), whole(2 * PANEL, F), whole(COLS, NRESP), whole(2, PANEL, PANEL)],
        out_specs=(pl.BlockSpec((BLK, COLS), lambda b: (b, 0)), pl.BlockSpec((BLK, NRESP), lambda b: (b, 0))),
        scratch_shapes=[pltpu.VMEM((PANEL, PANEL), BF), pltpu.VMEM((COLS, 2 * PANEL), BF), pltpu.VMEM((1, 2 * PANEL), F32),
                        pltpu.VMEM((1, COLS), F32), pltpu.VMEM((2, PANEL, PANEL), BF), pltpu.VMEM((2, PANEL, PANEL), BF)],
        compiler_params=pltpu.CompilerParams(dimension_semantics=("arbitrary",), vmem_limit_bytes=50 << 20),
        name="tile",
    )(xr, xc, xp, coef, w)


def reduce_kernel(part, targets, res, sbuf, rbuf, pbuf, ssem, s1, s2):
    x, l, h, z, k = place()
    sib = device(x, l, h, z, 1 - k)
    peers = [((z + i // 2) % 8, (h + i) % 2) for i in range(16)]
    bar = pltpu.get_barrier_semaphore()
    for i in range(1, 16):
        zz, hh = peers[i]
        pl.semaphore_signal(bar, inc=1, device_id=device(x, l, hh, zz, k), device_id_type=MESH)
    pl.semaphore_signal(bar, inc=1, device_id=sib, device_id_type=MESH)
    pl.semaphore_wait(bar, 16)
    out = Sender(ssem)
    order = [4, 5, 3, 6, 2, 7, 1, 0]
    for d in order:
        zz = (z + d) % 8
        out.send(part.at[zz, :, 1 - k], pbuf.at[zz], s1.at[d], sib)
    for d in order:
        zz = (z + d) % 8
        pltpu.make_async_copy(pbuf.at[zz], pbuf.at[zz], s1.at[d]).wait()
        for i in (2 * d, 2 * d + 1):
            hh = (h + i) % 2
            total = part[zz, hh, k] + pbuf[zz, hh]
            sbuf[i] = total.astype(BF)
            if i > 0:
                out.send(sbuf.at[i], rbuf.at[i], s2.at[i], device(x, l, hh, zz, k))
    acc = targets[...] - sbuf[0].astype(F32)
    for i in range(1, 16):
        pltpu.make_async_copy(rbuf.at[i], rbuf.at[i], s2.at[i]).wait()
        acc = acc - rbuf[i].astype(F32)
    res[...] = acc
    out.drain()


def reduce(part, targets):
    dma = pltpu.SemaphoreType.DMA
    vm = pl.BlockSpec(memory_space=pltpu.VMEM)
    return pl.pallas_call(
        reduce_kernel,
        out_shape=jax.ShapeDtypeStruct((SHARD, NRESP), F32),
        in_specs=[vm, vm],
        out_specs=vm,
        scratch_shapes=[pltpu.VMEM((16, SHARD, NRESP), BF), pltpu.VMEM((16, SHARD, NRESP), BF), pltpu.VMEM((8, 2, SHARD, NRESP), F32),
                        dma((40,)), dma((8,)), dma((16,))],
        compiler_params=pltpu.CompilerParams(collective_id=1, has_side_effects=True, vmem_limit_bytes=40 << 20),
        name="reduce",
    )(part.reshape(8, 2, 2, SHARD, NRESP), targets)


def body(descriptors, coefficients, targets, whitening):
    xr, xc, xp = gather(descriptors)
    updated, part = tile(xr, xc, xp.reshape(2 * PANEL, F), coefficients, whitening)
    return updated, reduce(part, targets)


def solution(mesh):
    in_specs = (P(("row", "col"), None), P("col", None), P(("row", "col"), None), P())
    out_specs = (P("row", "col"), P(("row", "col"), None))
    return jax.shard_map(body, mesh=mesh, in_specs=in_specs, out_specs=out_specs, check_vma=False)
```

time: 1240 us -> 148 us (0.12)
  the two profiles are of different devices: /device:TPU:70 before, /device:TPU:1 now
where the time goes in v1:
time: 148 us
  Pallas kernels  140 us (95%)
  local copies, waits for them, and re-layouts  7.61 us (5%)
    pallas_call x1, Pallas kernels, gather(): pl.pallas_call(gather_kernel, out_shape=(jax.ShapeDtypeStruct((ROWS, F),...  68.9 us
    pallas_call x1, Pallas kernels, reduce(): pl.pallas_call(reduce_kernel, out_shape=jax.ShapeDtypeStruct((SHARD, NRES...  47.2 us
    pallas_call x1, Pallas kernels, tile(): pl.pallas_call(tile_kernel, grid=(ROWS // BLK,), out_shape=(jax.ShapeDtyp...  23.5 us
    unnamed x13, local copies, waits for them, and re-layouts  7.61 us

profile of v1, /device:TPU:1, one launch (start us, length us, event | category | flops | bytes accessed | tf_op | source)
XLA Modules:
  0.0 147.9 jit_solution(9387554865009856017)
XLA Ops:
  0.6 0.0 copy-start.4
  0.6 0.9 copy-done.4
  1.5 0.0 copy-start.5
  1.5 68.9 %gather.1 = (bf16[3072,768]{1,0:T(8,128)(2,1)S(1)}, bf16[768,768]{1,0:T(8,128)(2,1)S(1)}, bf16[8,2,2,16,768]{4,3,2,1,0:T(8,128)(2,1)S(1)}) custom-call(bf16[96,768]{1,0:T(8,128)(2,1)S(1)} %copy-done.4), custom_call_target="tpu_custom_call" | custom-call | tf_op jit(solution)/shard_map/gather/pallas_call | solution.py:279
  70.5 0.0 copy-start
  70.5 2.1 %copy-done = bf16[3072,768]{1,0:T(8,128)(2,1)} copy-done((bf16[3072,768]{1,0:T(8,128)(2,1)}, bf16[3072,768]{1,0:T(8,128)(2,1)S(1)}, u32[]{:S(2)}) %copy-start) | copy-done | bytes 4718616
  72.6 0.0 copy-start.2
  72.6 1.0 copy-done.2
  73.7 0.0 copy-start.3
  73.7 1.0 copy-done.3
  74.7 23.5 %tile.1 = (f32[3072,768]{1,0:T(8,128)}, f32[3072,256]{1,0:T(8,128)}) custom-call(bf16[3072,768]{1,0:T(8,128)(2,1)} %copy-done, bf16[768,768]{1,0:T(8,128)(2,1)S(1)} %get-tuple-element.8.xc, bf16[512,768]{1,0:T(8,128)(2,1)S(1)} %bitcast.3, bf16[768,256]{1,0:T(8,128)(2,1)S(1)} %copy-done.3, f32[2,256,256]{2,1,0:T(8,128)S(1)} %copy-done.2), custom_call_target="tpu_custom_call" | custom-call | tf_op jit(solution)/shard_map/tile/pallas_call | solution.py:380
  98.2 0.0 copy-done.5
  98.2 0.0 copy-start.1
  98.2 1.9 %copy-done.1 = f32[3072,256]{1,0:T(8,128)S(1)} copy-done((f32[3072,256]{1,0:T(8,128)S(1)}, f32[3072,256]{1,0:T(8,128)}, u32[]{:S(2)}) %copy-start.1) | copy-done | bytes 3145752
  100.1 47.2 %reduce.1 = f32[96,256]{1,0:T(8,128)S(1)} custom-call(f32[8,2,2,96,256]{4,3,2,1,0:T(8,128)S(1)} %bitcast.2, f32[96,256]{1,0:T(8,128)S(1)} %copy-done.5), custom_call_target="tpu_custom_call" | custom-call | tf_op jit(solution)/shard_map/reduce/pallas_call | solution.py:428
  147.3 0.6 copy.7
Async XLA Ops:
  0.6 0.9 copy-start.4
  1.5 96.7 %copy-start.5 = (f32[96,256]{1,0:T(8,128)S(1)}, f32[96,256]{1,0:T(8,128)}, u32[]{:S(2)}) copy-start(f32[96,256]{1,0:T(8,128)} %targets.1) | copy-start | bytes 294916
  70.5 2.1 %copy-start = (bf16[3072,768]{1,0:T(8,128)(2,1)}, bf16[3072,768]{1,0:T(8,128)(2,1)S(1)}, u32[]{:S(2)}) copy-start(bf16[3072,768]{1,0:T(8,128)(2,1)S(1)} %get-tuple-element.7.xr) | copy-start | bytes 14155780
  72.6 1.0 copy-start.2
  73.7 1.0 copy-start.3
  98.2 1.9 %copy-start.1 = (f32[3072,256]{1,0:T(8,128)S(1)}, f32[3072,256]{1,0:T(8,128)}, u32[]{:S(2)}) copy-start(f32[3072,256]{1,0:T(8,128)} %get-tuple-element.11) | copy-start | bytes 9437188

commit v2 on v0

v2 whole, which is shorter than its diff:
```python
import jax
import jax.numpy as jnp
from jax import lax
from jax.experimental import pallas as pl
from jax.experimental.pallas import tpu as pltpu
from jax.sharding import PartitionSpec as P

MESH = pl.DeviceIdType.MESH
SHARD, F = 96, 768
ROWS, COLS = 3072, 768
RIDGE = 0.5
NRESP = 256
PANEL = 256
BLK = 384
HALF = 48
BF, F32 = jnp.bfloat16, jnp.float32


def place():
    r = lax.axis_index("row")
    c = lax.axis_index("col")
    return r % 4, r // 4, (c // 2) % 2, c // 4, c % 2


def device(x, l, h, z, k):
    return (l * 4 + x, z * 4 + h * 2 + k)


def both(*conds):
    out = conds[0]
    for cond in conds[1:]:
        out = jnp.logical_and(out, cond)
    return out


def dot_t(a, b):
    return lax.dot_general(a, b, (((1,), (1,)), ((), ())), preferred_element_type=F32)


def dot(a, b):
    return jnp.dot(a, b, preferred_element_type=F32)


def halves(a):
    high = a.astype(BF)
    return high, (a - high.astype(F32)).astype(BF)


def whiten(values, w_high, w_low):
    high, low = halves(values)
    return (dot(high, w_high) + dot(high, w_low) + dot(low, w_high)).astype(BF)


def square_sums(points):
    wide = points.astype(F32)
    return jnp.sum(wide * wide, axis=1, keepdims=True)


def as_row(column):
    n = column.shape[0]
    return jnp.transpose(jnp.broadcast_to(column, (n, 128)))[0:1, :]


def gaussian(left, right, left_sums, right_sums):
    distance = left_sums + right_sums - 2.0 * dot_t(left, right)
    return jnp.exp(distance * (-1.0 / (2.0 * F)))


def with_ridge(values, gap):
    i = lax.broadcasted_iota(jnp.int32, values.shape, 0)
    j = lax.broadcasted_iota(jnp.int32, values.shape, 1)
    return values + jnp.where(i - j == gap, RIDGE, 0.0)


class Sender:
    def __init__(self, sems):
        self.sems = sems
        self.items = []

    def send(self, src, dst, recv, dev, cond=None):
        n = len(self.items)

        def make():
            return pltpu.make_async_remote_copy(
                src, dst, self.sems.at[n], recv, device_id=dev, device_id_type=MESH
            )

        self.items.append((make, cond))
        if cond is None:
            make().start()
        else:
            pl.when(cond)(lambda: make().start())

    def drain(self):
        for make, cond in self.items:
            if cond is None:
                make().wait_send()
            else:
                pl.when(cond)(lambda make=make: make().wait_send())


def arrived(ref, sem, cond=None):
    def wait():
        pltpu.make_async_copy(ref, ref, sem).wait()

    if cond is None:
        wait()
    else:
        pl.when(cond)(wait)


def main_kernel(
    x_in, coef_in, w_in, t_in,
    kern, pr, pc, res,
    xr, xc, xp, coef, w, t, top, sp, sj, wh, wl, part, pbuf, sbuf, rbuf,
    ssem, za, yb, yc, sa, sb, sc, xps, xms, yx, op, om, op2, om2, xsend, p1, p2, p3, loc, s1, s1s, s2, s2s,
):
    x, l, h, z, k = place()
    r = l * 4 + x
    c = z * 4 + h * 2 + k
    zplus, zminus = device(x, l, h, (z + 1) % 8, k), device(x, l, h, (z + 7) % 8, k)
    ypart, sib = device(x, l, 1 - h, z, k), device(x, l, h, z, 1 - k)
    xplus, xminus = device((x + 1) % 4, l, h, z, k), device((x + 3) % 4, l, h, z, k)
    yl = device(x, 1 - l, h, z, k)
    t_of_me = 4 * r + 2 * h + k
    is_owner = both(r == 0, c < 6)
    self_piece = both(r == 0, c == 0)
    not_self = jnp.logical_not(self_piece)

    def first(p, hh, kk):
        return 384 * p + 96 * (2 * hh + kk)

    def rows(start, n):
        return xr.at[pl.ds(pl.multiple_of(start, 16), n)]

    own = first(z, h, k)
    fetches = [
        pltpu.make_async_copy(x_in, rows(own, 96), loc.at[0]),
        pltpu.make_async_copy(coef_in, coef, loc.at[1]),
        pltpu.make_async_copy(w_in, w, loc.at[2]),
        pltpu.make_async_copy(t_in, t, loc.at[3]),
    ]
    for fetch in fetches:
        fetch.start()

    bar = pltpu.get_barrier_semaphore()

    def hello(dev):
        pl.semaphore_signal(bar, inc=1, device_id=dev, device_id_type=MESH)

    for i in range(1, 16):
        hello(((r + i // 2) % 8, z * 4 + ((h + i) % 2) * 2 + k))
    for i in range(2, 16):
        hello(device(x, l, (h + i) % 2, (z + i // 2) % 8, k))
    hello(sib)
    pl.when(not_self)(lambda: hello((0, t_of_me // 6)))
    extra = jnp.where(c == 0, 47, jnp.where(c < 5, 48, 16))
    pl.semaphore_wait(bar, 30 + jnp.where(is_owner, extra, 0))

    out = Sender(ssem)

    def piece(p, n):
        return rows(first(p, h, k) + HALF * n if n < 2 else first(p, 1 - h, k), HALF)

    def plane(s, d):
        return (z + 16 - d * s) % 8

    def slot(s, n):
        return 0 if s == 0 else 2 * s - 1 + n

    first_copy = fetches[0]
    mine = [x_in.at[pl.ds(HALF * n, HALF)] for n in range(2)]
    out.send(mine[0], piece(z, 0), yb.at[0], ypart)
    for n in range(2):
        out.send(mine[n], piece(z, n), za.at[n], zplus)
        out.send(mine[n], piece(z, n), za.at[3 + n], zminus)
    out.send(mine[1], piece(z, 1), yc.at[0], ypart)
    out.send(x_in, rows(own, 96), sa.at[0], sib)
    arrived(piece(z, 2), yb.at[0])
    out.send(piece(z, 2), piece(z, 2), za.at[2], zplus)
    out.send(piece(z, 2), piece(z, 2), za.at[5], zminus)
    out.send(piece(z, 2), piece(z, 2), sb.at[0], sib)

    def late(s):
        pairs = [(n, d) for n, d in enumerate((1, -1)) if not (s in (0, 4) and n == 1)]
        for n, d in pairs:
            i, p = slot(s, n), plane(s, d)
            got = rows(first(p, 1 - h, k) + HALF, HALF)
            arrived(got, yc.at[i])
            out.send(got, got, sc.at[i], sib)
        for n, d in pairs:
            i, p = slot(s, n), plane(s, d)
            arrived(rows(first(p, h, 1 - k), 96), sa.at[i])
            arrived(rows(first(p, 1 - h, 1 - k), HALF), sb.at[i])
            arrived(rows(first(p, 1 - h, 1 - k) + HALF, HALF), sc.at[i])

    xs, ls = z % 4, z // 4
    q = (x + 4 - xs) % 4
    line = l == ls
    other = jnp.logical_not(line)
    hops_plus, hops_minus = q, (4 - q) % 4
    near = jnp.minimum(q, 4 - q)
    b0, bm, bp, bo = (q + 3) % 4, (q + 2) % 4, q, (q + 1) % 4

    def gap(j):
        away = (4 * h + 2 * k + j + 8 - z) % 8
        return jnp.minimum(away, 8 - away)

    def block(j, b, half=None):
        start = 384 * j + 96 * b + (0 if half is None else HALF * half)
        return xc.at[pl.ds(pl.multiple_of(start, 16), 96 if half is None else HALF)]

    def raw(j, b):
        return rows(384 * (4 * h + 2 * k + j) + 96 * b, 96)

    def remote(src, dst, n, recv, dev):
        return pltpu.make_async_remote_copy(src, dst, xsend.at[n], recv, device_id=dev, device_id_type=MESH)

    def column_stage(s):
        def step(j, carry):
            g = gap(j)

            @pl.when(both(line, g + hops_plus == s))
            def _():
                for u in range(2):
                    got = block(j, u)
                    arrived(got, xps.at[2 * j + u], q != 0)

                    @pl.when(q == 0)
                    def _():
                        remote(raw(j, u), got, 5 * j + u, xps.at[2 * j + u], xplus).start()

                    @pl.when(both(q != 0, q != 3))
                    def _():
                        remote(got, got, 5 * j + u, xps.at[2 * j + u], xplus).start()

                    @pl.when(q == u + 1)
                    def _():
                        remote(got, got, 5 * j + 4, yx.at[j], yl).start()

            @pl.when(both(line, g + hops_minus == s))
            def _():
                for u in range(2):
                    got = block(j, 2 + u)
                    arrived(got, xms.at[2 * j + u], q != 0)

                    @pl.when(q == 0)
                    def _():
                        remote(raw(j, 2 + u), got, 5 * j + 2 + u, xms.at[2 * j + u], xminus).start()

                    @pl.when(both(q != 0, q != 1))
                    def _():
                        remote(got, got, 5 * j + 2 + u, xms.at[2 * j + u], xminus).start()

                    if u == 0:
                        @pl.when(q == 3)
                        def _():
                            remote(got, got, 5 * j + 4, yx.at[j], yl).start()
                    else:
                        @pl.when(q == 0)
                        def _():
                            remote(raw(j, 3), got, 5 * j + 4, yx.at[j], yl).start()

            @pl.when(both(other, g + near + 1 == s))
            def _():
                got = block(j, b0)
                arrived(got, yx.at[j])
                remote(got, got, 5 * j, op.at[j], xplus).start()
                remote(got, got, 5 * j + 1, om.at[j], xminus).start()

            @pl.when(both(other, g + jnp.where(q % 2 == 0, 3, 4) == s))
            def _():
                arrived(block(j, bm), op.at[j])
                remote(block(j, bm, 0), block(j, bm, 0), 5 * j + 2, op2.at[j], xplus).start()
                arrived(block(j, bp), om.at[j])
                remote(block(j, bp, 1), block(j, bp, 1), 5 * j + 3, om2.at[j], xminus).start()

            return carry

        lax.fori_loop(0, 2, step, 0)

    def columns_end():
        def step(j, carry):
            @pl.when(other)
            def _():
                arrived(block(j, bo, 0), op2.at[j])
                arrived(block(j, bo, 1), om2.at[j])
                remote(block(j, 0), block(j, 0), 5 * j, op.at[j], xplus).wait_send()
                remote(block(j, 0), block(j, 0), 5 * j + 1, om.at[j], xminus).wait_send()
                remote(block(j, 0, 0), block(j, 0, 0), 5 * j + 2, op2.at[j], xplus).wait_send()
                remote(block(j, 0, 0), block(j, 0, 0), 5 * j + 3, om2.at[j], xminus).wait_send()

            for u in range(2):
                @pl.when(both(line, q != 3))
                def _():
                    remote(block(j, u), block(j, u), 5 * j + u, xps.at[0], xplus).wait_send()

                @pl.when(both(line, q != 1))
                def _():
                    remote(block(j, u), block(j, u), 5 * j + 2 + u, xms.at[0], xminus).wait_send()

            @pl.when(line)
            def _():
                remote(block(j, 0), block(j, 0), 5 * j + 4, yx.at[0], yl).wait_send()

            return carry

        lax.fori_loop(0, 2, step, 0)

    def panel_points_out():
        for j in range(6):
            tt = 6 * c + j
            has = both(is_owner, tt < 32)
            for zz in range(8):
                out.send(
                    x_in.at[pl.ds(16 * j, 16)],
                    xp.at[tt // 4, (tt // 2) % 2, tt % 2],
                    p1.at[0],
                    (tt // 4, zz * 4 + tt % 4),
                    both(has, jnp.logical_or(tt > 0, z != zz)) if (j == 0 and zz == 0) else has,
                )

        @pl.when(self_piece)
        def _():
            keep = pltpu.make_async_copy(x_in.at[pl.ds(0, 16)], xp.at[0, 0, 0], loc.at[4])
            keep.start()
            keep.wait()

    def panel_points_plane():
        got = xp.at[r, h, k]
        arrived(got, p1.at[0], not_self)
        for i in range(1, 16):
            out.send(got, got, p2.at[i - 1], ((r + i // 2) % 8, z * 4 + ((h + i) % 2) * 2 + k))

    def panel_points_chip():
        for i in range(1, 16):
            arrived(xp.at[(r + 8 - i // 2) % 8, (h + i) % 2, k], p2.at[i - 1])
        got = xp.at[:, :, k]
        out.send(got, got, p3.at[0], sib)

    for s in range(1, 5):
        if s < 4:
            for n in range(3):
                for e, d in enumerate((1, -1)):
                    got = piece(plane(s, d), n)
                    i = slot(s, e)
                    arrived(got, za.at[6 * (s - 1) + 3 * e + n])
                    if s < 3:
                        out.send(got, got, za.at[6 * s + 3 * e + n], zplus if d == 1 else zminus)
                    if n == 1:
                        out.send(got, got, yc.at[i], ypart)
                        whole = rows(first(plane(s, d), h, k), 96)
                        out.send(whole, whole, sa.at[i], sib)
                    if n == 2:
                        out.send(got, got, sb.at[i], sib)
                if s == 3:
                    d = (1 - 2 * k) if n < 2 else (2 * k - 1)
                    got = piece((z + 16 - 3 * d) % 8, n)
                    out.send(got, got, za.at[18 + n], device(x, l, h, (z + 8 + d) % 8, k))
        else:
            for n in range(3):
                got = piece(plane(4, 1), n)
                arrived(got, za.at[18 + n])
                if n == 1:
                    out.send(got, got, yc.at[7], ypart)
                    whole = rows(first(plane(4, 1), h, k), 96)
                    out.send(whole, whole, sa.at[7], sib)
                if n == 2:
                    out.send(got, got, sb.at[7], sib)
        if s == 1:
            panel_points_out()
            first_copy.wait()
        late(s - 1)
        column_stage(s - 1)
        if s == 3:
            panel_points_plane()
    late(4)
    keep = pltpu.make_async_copy(rows(768 * (2 * h + k), 768), xc, loc.at[4])
    source = both(line, q == 0)
    column_stage(4)
    pl.when(source)(lambda: keep.start())
    for fetch in fetches[1:]:
        fetch.wait()
    for i in range(2):
        high, low = halves(w[i])
        wh[i] = high
        wl[i] = low
    for s in range(5, 9):
        column_stage(s)
    pl.when(source)(lambda: keep.wait())
    columns_end()
    panel_points_chip()

    sj[...] = as_row(square_sums(xc[...]))
    row_first = r * ROWS
    col_first = c * COLS

    def turn(i):
        return (4 + ((i + 1) // 2) * (2 * (i % 2) - 1)) % 8

    def to_sib(i):
        zz = (z + turn(i)) % 8
        return pltpu.make_async_remote_copy(
            part.at[zz, :, 1 - k], pbuf.at[zz], s1s.at[i], s1.at[i], device_id=sib, device_id_type=MESH
        )

    def to_owner(i, g):
        d = turn(i)
        zz = (z + d) % 8
        n = 2 * d + g
        return pltpu.make_async_remote_copy(
            sbuf.at[n], rbuf.at[n], s2s.at[n], s2.at[n], device_id=device(x, l, (h + g) % 2, zz, k), device_id_type=MESH
        )

    def exchange(i):
        @pl.when(both(i >= 1, i < 9))
        def _():
            to_sib(i - 1).start()

        @pl.when(both(i >= 3, i < 11))
        def _():
            for g in range(2):
                pl.when(jnp.logical_or(i != 10, g != 0))(lambda g=g: to_owner(i - 3, g).start())

    def chip_sum(i):
        @pl.when(both(i >= 2, i < 10))
        def _():
            d = turn(i - 2)
            zz = (z + d) % 8
            arrived(pbuf.at[zz], s1.at[i - 2])
            for g in range(2):
                hh = (h + g) % 2
                sbuf[2 * d + g] = (part[zz, hh, k] + pbuf[zz, hh]).astype(BF)

    def tile_step(i, carry):
        exchange(i)
        b = (z + turn(i)) % 8
        span = pl.ds(pl.multiple_of(b * BLK, BLK), BLK)
        points = xr[span, :]
        values = with_ridge(gaussian(points, xc[...], square_sums(points), sj[...]), col_first - row_first - b * BLK)
        kern[span, :] = values
        part[b] = dot(values.astype(BF), coef[...]).reshape(2, 2, SHARD, NRESP)
        chip_sum(i)
        return carry

    lax.fori_loop(0, 8, tile_step, 0)

    arrived(xp.at[:, :, 1 - k], p3.at[0])
    heads = xp.reshape(2 * PANEL, F)
    sp[...] = as_row(square_sums(heads[...]))
    lower = heads[PANEL:, :]
    top[...] = whiten(gaussian(lower, heads[:PANEL, :], square_sums(lower), sp[:, :PANEL]), wh[0], wl[0])

    def panels(points, start):
        k0 = with_ridge(gaussian(points, heads[...], square_sums(points), sp[...]), -start)
        p1 = whiten(k0[:, :PANEL], wh[0], wl[0])
        return p1, whiten(k0[:, PANEL:] - dot_t(p1, top[...]), wh[1], wl[1])

    def panel_step(b, carry):
        exchange(b + 8)
        span = pl.ds(pl.multiple_of(b * BLK, BLK), BLK)
        p1, p2 = panels(xr[span, :], row_first + b * BLK)
        pr[span, :PANEL] = p1
        pr[span, PANEL:] = p2
        chip_sum(b + 8)
        return carry

    lax.fori_loop(0, 8, panel_step, 0)

    def panel_cols(j, carry):
        span = pl.ds(pl.multiple_of(j * BLK, BLK), BLK)
        p1, p2 = panels(xc[span, :], col_first + j * BLK)
        pc[span, :PANEL] = p1
        pc[span, PANEL:] = p2
        return carry

    lax.fori_loop(0, 2, panel_cols, 0)

    acc = t[...] - sbuf[0].astype(F32)
    for n in range(2, 16):
        arrived(rbuf.at[n], s2.at[n])
        acc = acc - rbuf[n].astype(F32)
    arrived(rbuf.at[1], s2.at[1])
    res[...] = acc - rbuf[1].astype(F32)
    for i in range(8):
        to_sib(i).wait_send()
        for g in range(2):
            if i != 7 or g != 0:
                to_owner(i, g).wait_send()
    out.drain()


def update_kernel(kern, pr, pc, upd, buf, sem):
    def copy(b, n):
        return pltpu.make_async_copy(buf.at[n], upd.at[pl.ds(pl.multiple_of(b * BLK, BLK), BLK)], sem.at[n])

    def step(b, carry):
        n = b % 2
        pl.when(b >= 2)(lambda: copy(b - 2, n).wait())
        span = pl.ds(pl.multiple_of(b * BLK, BLK), BLK)
        buf[n] = kern[span, :] - dot_t(pr[span, :PANEL], pc[:, :PANEL]) - dot_t(pr[span, PANEL:], pc[:, PANEL:])
        copy(b, n).start()
        return carry

    lax.fori_loop(0, 8, step, 0)
    copy(6, 0).wait()
    copy(7, 1).wait()


def body(descriptors, coefficients, targets, whitening):
    dma = pltpu.SemaphoreType.DMA
    vm = pl.BlockSpec(memory_space=pltpu.VMEM)
    hbm = pl.BlockSpec(memory_space=pltpu.HBM)
    V = pltpu.VMEM
    kern, pr, pc, residual = pl.pallas_call(
        main_kernel,
        out_shape=(
            jax.ShapeDtypeStruct((ROWS, COLS), F32),
            jax.ShapeDtypeStruct((ROWS, 2 * PANEL), BF),
            jax.ShapeDtypeStruct((COLS, 2 * PANEL), BF),
            jax.ShapeDtypeStruct((SHARD, NRESP), F32),
        ),
        in_specs=[hbm] * 4,
        out_specs=(vm, vm, vm, vm),
        scratch_shapes=[
            V((ROWS, F), BF), V((COLS, F), BF), V((8, 2, 2, 16, F), BF), V((COLS, NRESP), BF), V((2, PANEL, PANEL), F32),
            V((SHARD, NRESP), F32), V((PANEL, PANEL), BF), V((1, 2 * PANEL), F32), V((1, COLS), F32),
            V((2, PANEL, PANEL), BF), V((2, PANEL, PANEL), BF), V((8, 2, 2, SHARD, NRESP), F32),
            V((8, 2, SHARD, NRESP), F32), V((16, SHARD, NRESP), BF), V((16, SHARD, NRESP), BF),
            dma((180,)), dma((21,)), dma((1,)), dma((8,)), dma((8,)), dma((8,)), dma((8,)), dma((4,)), dma((4,)), dma((2,)),
            dma((2,)), dma((2,)), dma((2,)), dma((2,)), dma((10,)), dma((1,)), dma((15,)), dma((1,)), dma((5,)),
            dma((8,)), dma((8,)), dma((16,)), dma((16,)),
        ],
        compiler_params=pltpu.CompilerParams(collective_id=0, has_side_effects=True, vmem_limit_bytes=26 << 20),
        name="main",
    )(descriptors, coefficients, whitening, targets)
    updated = pl.pallas_call(
        update_kernel,
        out_shape=jax.ShapeDtypeStruct((ROWS, COLS), F32),
        in_specs=[vm] * 3,
        out_specs=hbm,
        scratch_shapes=[V((2, BLK, COLS), F32), dma((2,))],
        compiler_params=pltpu.CompilerParams(vmem_limit_bytes=16 << 20),
        name="update",
    )(kern, pr, pc)
    return updated, residual


def solution(mesh):
    in_specs = (P(("row", "col"), None), P("col", None), P(("row", "col"), None), P())
    out_specs = (P("row", "col"), P(("row", "col"), None))
    return jax.shard_map(body, mesh=mesh, in_specs=in_specs, out_specs=out_specs, check_vma=False)
```

time: 1240 us -> 113 us (0.09)
  the two profiles are of different devices: /device:TPU:70 before, /device:TPU:24 now
where the time goes in v2:
time: 113 us; the launch traced here: 112 us
  Pallas kernels  107 us (95%)
  local copies, waits for them, and re-layouts  4.47 us (4%)
    pallas_call x1, Pallas kernels, body(): pl.pallas_call(main_kernel, out_shape=(jax.ShapeDtypeStruct((ROWS, COLS),...  101 us
    pallas_call x1, Pallas kernels, body(): pl.pallas_call(update_kernel, out_shape=jax.ShapeDtypeStruct((ROWS, COLS)...  6.59 us
    unnamed x9, local copies, waits for them, and re-layouts  4.47 us

profile of v2, /device:TPU:24, one launch (start us, length us, event | category | flops | bytes accessed | tf_op | source)
XLA Modules:
  0.0 112.4 jit_solution(11369865427520159819)
XLA Ops:
  0.6 0.0 copy-start
  0.6 1.0 copy-done
  1.7 0.0 copy-start.1
  1.7 1.0 copy-done.1
  2.7 0.0 copy-start.2
  2.7 0.9 copy-done.2
  3.6 0.0 copy-start.3
  3.6 0.9 copy-done.3
  4.5 100.7 %main.1 = (f32[3072,768]{1,0:T(8,128)S(1)}, bf16[3072,512]{1,0:T(8,128)(2,1)S(1)}, bf16[768,512]{1,0:T(8,128)(2,1)S(1)}, f32[96,256]{1,0:T(8,128)S(1)}) custom-call(bf16[96,768]{1,0:T(8,128)(2,1)S(1)} %copy-done.2, bf16[768,256]{1,0:T(8,128)(2,1)S(1)} %copy-done.1, f32[2,256,256]{2,1,0:T(8,128)S(1)} %copy-done, f32[96,256]{1,0:T(8,128)S(1)} %copy-done.3), custom_call_target="tpu_custom_call" | custom-call | tf_op jit(solution)/shard_map/main/pallas_call | solution.py:515
  105.2 6.6 %update.1 = f32[3072,768]{1,0:T(8,128)} custom-call(f32[3072,768]{1,0:T(8,128)S(1)} %get-tuple-element.6.kern, bf16[3072,512]{1,0:T(8,128)(2,1)S(1)} %get-tuple-element.7.pr, bf16[768,512]{1,0:T(8,128)(2,1)S(1)} %get-tuple-element.8.pc), custom_call_target="tpu_custom_call" | custom-call | tf_op jit(solution)/shard_map/update/pallas_call | solution.py:537
  111.8 0.6 copy.7
Async XLA Ops:
  0.6 1.0 copy-start
  1.7 1.0 copy-start.1
  2.7 0.9 copy-start.2
  3.6 0.9 copy-start.3

commit v3 on v2

v3 whole, which is shorter than its diff:
```python
import jax
import jax.numpy as jnp
from jax import lax
from jax.experimental import pallas as pl
from jax.experimental.pallas import tpu as pltpu
from jax.sharding import PartitionSpec as P

MESH = pl.DeviceIdType.MESH
SHARD, F = 96, 768
ROWS, COLS = 3072, 768
RIDGE = 0.5
NRESP = 256
PANEL = 256
BLK = 384
HALF = 48
BF, F32 = jnp.bfloat16, jnp.float32
SCALE = 1.4426950408889634 / (2.0 * F)


def place():
    r = lax.axis_index("row")
    c = lax.axis_index("col")
    return r % 4, r // 4, (c // 2) % 2, c // 4, c % 2


def device(x, l, h, z, k):
    return (l * 4 + x, z * 4 + h * 2 + k)


def both(*conds):
    out = conds[0]
    for cond in conds[1:]:
        out = jnp.logical_and(out, cond)
    return out


def dot_t(a, b):
    return lax.dot_general(a, b, (((1,), (1,)), ((), ())), preferred_element_type=F32)


def dot(a, b):
    return jnp.dot(a, b, preferred_element_type=F32)


def halves(a):
    high = a.astype(BF)
    return high, (a - high.astype(F32)).astype(BF)


def whiten(values, w_high, w_low):
    high, low = halves(values)
    return (dot(high, w_high) + dot(high, w_low) + dot(low, w_high)).astype(BF)


def square_sums(points):
    wide = points.astype(F32)
    return jnp.sum(wide * wide, axis=1, keepdims=True) * -SCALE


def as_row(column):
    n = column.shape[0]
    return jnp.transpose(jnp.broadcast_to(column, (n, 128)))[0:1, :]


def gaussian(left, right, left_sums, right_sums):
    return jnp.exp2((2.0 * SCALE) * dot_t(left, right) + (left_sums + right_sums))


def add_ridge(ref, span, gap):
    shape = (BLK, ref.shape[1])

    @pl.when(both(gap > -shape[1], gap < shape[0]))
    def _():
        i = lax.broadcasted_iota(jnp.int32, shape, 0)
        j = lax.broadcasted_iota(jnp.int32, shape, 1)
        ref[span, :] += jnp.where(i - j == gap, RIDGE, 0.0)


class Sender:
    def __init__(self, sems):
        self.sems = sems
        self.items = []

    def send(self, src, dst, recv, dev, cond=None):
        n = len(self.items)

        def make():
            return pltpu.make_async_remote_copy(
                src, dst, self.sems.at[n], recv, device_id=dev, device_id_type=MESH
            )

        self.items.append((make, cond))
        if cond is None:
            make().start()
        else:
            pl.when(cond)(lambda: make().start())

    def drain(self):
        for make, cond in self.items:
            if cond is None:
                make().wait_send()
            else:
                pl.when(cond)(lambda make=make: make().wait_send())


def arrived(ref, sem, cond=None):
    def wait():
        pltpu.make_async_copy(ref, ref, sem).wait()

    if cond is None:
        wait()
    else:
        pl.when(cond)(wait)


def main_kernel(
    x_in, coef_in, w_in, t_in,
    kern, res,
    pr, pc, xr, xc, xp, coef, w, t, top, sp, sj, wh, wl, k0, part, pbuf, ybuf, yrecv, sbuf, rbuf,
    ssem, za, yb, yc, sa, sb, sc, xps, xms, yx, op, om, op2, xsend, p1, p2, p3, loc, s1, s1s, s3, s3s, s2, s2s, s4, s4s,
):
    x, l, h, z, k = place()
    r = l * 4 + x
    c = z * 4 + h * 2 + k
    zplus, zminus = device(x, l, h, (z + 1) % 8, k), device(x, l, h, (z + 7) % 8, k)
    ypart, sib = device(x, l, 1 - h, z, k), device(x, l, h, z, 1 - k)
    xplus, xminus = device((x + 1) % 4, l, h, z, k), device((x + 3) % 4, l, h, z, k)
    yl = device(x, 1 - l, h, z, k)
    t_of_me = 4 * r + 2 * h + k
    is_owner = both(r == 0, c < 6)
    self_piece = both(r == 0, c == 0)
    not_self = jnp.logical_not(self_piece)
    is_place = z == jnp.where(t_of_me < 24, 0, 1)

    def first(p, hh, kk):
        return 384 * p + 96 * (2 * hh + kk)

    def rows(start, n):
        return xr.at[pl.ds(pl.multiple_of(start, 16), n)]

    own = first(z, h, k)
    fetches = [
        pltpu.make_async_copy(x_in, rows(own, 96), loc.at[0]),
        pltpu.make_async_copy(coef_in, coef, loc.at[1]),
        pltpu.make_async_copy(w_in, w, loc.at[2]),
        pltpu.make_async_copy(t_in, t, loc.at[3]),
    ]
    for fetch in fetches:
        fetch.start()

    bar = pltpu.get_barrier_semaphore()

    def hello(dev):
        pl.semaphore_signal(bar, inc=1, device_id=dev, device_id_type=MESH)

    for i in range(1, 16):
        hello(((r + i // 2) % 8, z * 4 + ((h + i) % 2) * 2 + k))
    for i in range(2, 16):
        hello(device(x, l, (h + i) % 2, (z + i // 2) % 8, k))
    hello(sib)
    pl.when(both(is_place, not_self))(lambda: hello((0, t_of_me // 6)))
    extra = jnp.where(c == 0, 5, jnp.where(c < 5, 6, 2))
    pl.semaphore_wait(bar, 30 + jnp.where(is_owner, extra, 0))

    out = Sender(ssem)

    def piece(p, n):
        return rows(first(p, h, k) + HALF * n if n < 2 else first(p, 1 - h, k), HALF)

    def plane(s, d):
        return (z + 16 - d * s) % 8

    def slot(s, n):
        return 0 if s == 0 else 2 * s - 1 + n

    first_copy = fetches[0]
    mine = [x_in.at[pl.ds(HALF * n, HALF)] for n in range(2)]
    out.send(mine[0], piece(z, 0), yb.at[0], ypart)
    for n in range(2):
        out.send(mine[n], piece(z, n), za.at[n], zplus)
        out.send(mine[n], piece(z, n), za.at[3 + n], zminus)
    out.send(mine[1], piece(z, 1), yc.at[0], ypart)
    out.send(x_in, rows(own, 96), sa.at[0], sib)
    arrived(piece(z, 2), yb.at[0])
    out.send(piece(z, 2), piece(z, 2), za.at[2], zplus)
    out.send(piece(z, 2), piece(z, 2), za.at[5], zminus)
    out.send(piece(z, 2), piece(z, 2), sb.at[0], sib)

    def late(s):
        pairs = [(n, d) for n, d in enumerate((1, -1)) if not (s in (0, 4) and n == 1)]
        for n, d in pairs:
            i, p = slot(s, n), plane(s, d)
            got = rows(first(p, 1 - h, k) + HALF, HALF)
            arrived(got, yc.at[i])
            out.send(got, got, sc.at[i], sib)
        for n, d in pairs:
            i, p = slot(s, n), plane(s, d)
            arrived(rows(first(p, h, 1 - k), 96), sa.at[i])
            arrived(rows(first(p, 1 - h, 1 - k), HALF), sb.at[i])
            arrived(rows(first(p, 1 - h, 1 - k) + HALF, HALF), sc.at[i])

    xs, ls = z % 4, z // 4
    q = (x + 4 - xs) % 4
    line = l == ls
    other = jnp.logical_not(line)
    hops_plus, hops_minus = q, (4 - q) % 4
    b0, bm, bp, bo = (q + 3) % 4, (q + 2) % 4, q, (q + 1) % 4

    def gap(j):
        away = (4 * h + 2 * k + j + 8 - z) % 8
        return jnp.minimum(away, 8 - away)

    def block(j, b, half=None):
        start = 384 * j + 96 * b + (0 if half is None else HALF * half)
        return xc.at[pl.ds(pl.multiple_of(start, 16), 96 if half is None else HALF)]

    def raw(j, b):
        return rows(384 * (4 * h + 2 * k + j) + 96 * b, 96)

    def remote(src, dst, n, recv, dev):
        return pltpu.make_async_remote_copy(src, dst, xsend.at[n], recv, device_id=dev, device_id_type=MESH)

    across = device((x + 2) % 4, l, h, z, k)
    yl_across = device((x + 2) % 4, 1 - l, h, z, k)

    def part_of(ref, n):
        return ref.at[pl.ds(HALF * n, HALF)]

    def column_stage(s):
        def step(j, carry):
            g = gap(j)

            @pl.when(both(line, q == 0, g == s))
            def _():
                remote(raw(j, 3), block(j, 3), 10 * j + 8, yx.at[j], yl).start()
                remote(raw(j, 1), block(j, 1), 10 * j + 9, yx.at[j], yl_across).start()
                for u in range(4):
                    b, half = u // 2, u % 2
                    remote(part_of(raw(j, b), half), block(j, b, half), 10 * j + u, xps.at[4 * j + u], xplus).start()
                    b = 2 + b
                    remote(part_of(raw(j, b), half), block(j, b, half), 10 * j + 4 + u, xms.at[4 * j + u], xminus).start()

            @pl.when(both(line, q != 0, g + hops_plus == s))
            def _():
                for u in range(4):
                    got = block(j, u // 2, u % 2)
                    arrived(got, xps.at[4 * j + u])
                    pl.when(q != 3)(lambda: remote(got, got, 10 * j + u, xps.at[4 * j + u], xplus).start())
                    if u == 1:
                        pl.when(q == 1)(lambda: remote(block(j, 0), block(j, 0), 10 * j + 8, yx.at[j], yl).start())

            @pl.when(both(line, q != 0, g + hops_minus == s))
            def _():
                for u in range(4):
                    got = block(j, 2 + u // 2, u % 2)
                    arrived(got, xms.at[4 * j + u])
                    pl.when(q != 1)(lambda: remote(got, got, 10 * j + 4 + u, xms.at[4 * j + u], xminus).start())
                    if u == 1:
                        pl.when(q == 3)(lambda: remote(block(j, 2), block(j, 2), 10 * j + 8, yx.at[j], yl).start())

            @pl.when(both(other, g + 1 + q % 2 == s))
            def _():
                got = block(j, b0)
                arrived(got, yx.at[j])
                remote(got, got, 10 * j, op.at[j], xplus).start()
                remote(got, got, 10 * j + 1, om.at[j], xminus).start()
                remote(got, got, 10 * j + 2, op2.at[j], across).start()

            return carry

        lax.fori_loop(0, 2, step, 0)

    def columns_end():
        def step(j, carry):
            @pl.when(other)
            def _():
                arrived(block(j, bm), op.at[j])
                arrived(block(j, bp), om.at[j])
                arrived(block(j, bo), op2.at[j])
                for n in range(3):
                    remote(block(j, 0), block(j, 0), 10 * j + n, op.at[0], xplus).wait_send()

            for u in range(4):
                piece_of = block(j, 0, 0)
                pl.when(both(line, q != 3))(lambda: remote(piece_of, piece_of, 10 * j + u, xps.at[0], xplus).wait_send())
                pl.when(both(line, q != 1))(lambda: remote(piece_of, piece_of, 10 * j + 4 + u, xms.at[0], xminus).wait_send())
            pl.when(both(line, q != 2))(lambda: remote(block(j, 0), block(j, 0), 10 * j + 8, yx.at[0], yl).wait_send())
            pl.when(both(line, q == 0))(lambda: remote(block(j, 0), block(j, 0), 10 * j + 9, yx.at[0], yl).wait_send())
            return carry

        lax.fori_loop(0, 2, step, 0)

    def panel_points_out():
        for j in range(6):
            tt = 6 * c + j
            has = both(is_owner, tt < 32)
            out.send(
                x_in.at[pl.ds(16 * j, 16)],
                xp.at[tt // 4, (tt // 2) % 2, tt % 2],
                p1.at[0],
                (tt // 4, jnp.where(tt < 24, 0, 4) + tt % 4),
                both(has, tt > 0) if j == 0 else has,
            )

        @pl.when(self_piece)
        def _():
            keep = pltpu.make_async_copy(x_in.at[pl.ds(0, 16)], xp.at[0, 0, 0], loc.at[4])
            keep.start()
            keep.wait()

    def panel_points_planes():
        got = xp.at[r, h, k]
        arrived(got, p1.at[0], both(is_place, not_self))
        for i in range(1, 8):
            out.send(got, got, p1.at[0], device(x, l, h, (z + i) % 8, k), is_place)

    def panel_points_plane():
        got = xp.at[r, h, k]
        arrived(got, p1.at[0], jnp.logical_not(is_place))
        for i in range(1, 16):
            out.send(got, got, p2.at[i - 1], ((r + i // 2) % 8, z * 4 + ((h + i) % 2) * 2 + k))

    def panel_points_chip():
        for i in range(1, 16):
            arrived(xp.at[(r + 8 - i // 2) % 8, (h + i) % 2, k], p2.at[i - 1])
        got = xp.at[:, :, k]
        out.send(got, got, p3.at[0], sib)

    for s in range(1, 5):
        if s < 4:
            for n in range(3):
                for e, d in enumerate((1, -1)):
                    got = piece(plane(s, d), n)
                    i = slot(s, e)
                    arrived(got, za.at[6 * (s - 1) + 3 * e + n])
                    if s < 3:
                        out.send(got, got, za.at[6 * s + 3 * e + n], zplus if d == 1 else zminus)
                    if n == 1:
                        out.send(got, got, yc.at[i], ypart)
                        whole = rows(first(plane(s, d), h, k), 96)
                        out.send(whole, whole, sa.at[i], sib)
                    if n == 2:
                        out.send(got, got, sb.at[i], sib)
                if s == 3:
                    d = (1 - 2 * k) if n < 2 else (2 * k - 1)
                    got = piece((z + 16 - 3 * d) % 8, n)
                    out.send(got, got, za.at[18 + n], device(x, l, h, (z + 8 + d) % 8, k))
        else:
            for n in range(3):
                got = piece(plane(4, 1), n)
                arrived(got, za.at[18 + n])
                if n == 1:
                    out.send(got, got, yc.at[7], ypart)
                    whole = rows(first(plane(4, 1), h, k), 96)
                    out.send(whole, whole, sa.at[7], sib)
                if n == 2:
                    out.send(got, got, sb.at[7], sib)
        if s == 1:
            panel_points_out()
            first_copy.wait()
        if s == 2:
            panel_points_planes()
        late(s - 1)
        column_stage(s - 1)
    panel_points_plane()
    late(4)
    keep = pltpu.make_async_copy(rows(768 * (2 * h + k), 768), xc, loc.at[4])
    source = both(line, q == 0)
    column_stage(4)
    pl.when(source)(lambda: keep.start())
    for fetch in fetches[1:]:
        fetch.wait()
    for i in range(2):
        high, low = halves(w[i])
        wh[i] = high
        wl[i] = low
    panel_points_chip()
    row_first = r * ROWS
    col_first = c * COLS
    heads = xp.reshape(2 * PANEL, F)

    def panels(points, start):
        k0[...] = gaussian(points, heads[...], square_sums(points), sp[...])
        add_ridge(k0, pl.ds(0, BLK), -start)
        p1 = whiten(k0[:, :PANEL], wh[0], wl[0])
        return p1, whiten(k0[:, PANEL:] - dot_t(p1, top[...]), wh[1], wl[1])

    def panel_rows(b):
        span = pl.ds(pl.multiple_of(b * BLK, BLK), BLK)
        p1, p2 = panels(xr[span, :], row_first + b * BLK)
        pr[span, :PANEL] = p1
        pr[span, PANEL:] = p2

    column_stage(5)
    column_stage(6)
    arrived(xp.at[:, :, 1 - k], p3.at[0])
    sp[...] = as_row(square_sums(heads[...]))
    lower = heads[PANEL:, :]
    top[...] = whiten(gaussian(lower, heads[:PANEL, :], square_sums(lower), sp[:, :PANEL]), wh[0], wl[0])

    def panel_copy(b):
        rows_of = pr.at[pl.ds(pl.multiple_of(b * BLK, BLK), BLK)]
        return pltpu.make_async_remote_copy(
            rows_of, rows_of, s4s.at[b // 2], s4.at[b // 2], device_id=sib, device_id_type=MESH
        )

    def my_panels(n, carry):
        pl.when(n >= 1)(lambda: panel_copy(2 * n - 2 + k).start())
        panel_rows(2 * n + k)
        return carry

    lax.fori_loop(0, 4, my_panels, 0)
    column_stage(7)
    panel_copy(6 + k).start()
    pl.when(source)(lambda: keep.wait())
    columns_end()

    sj[...] = as_row(square_sums(xc[...]))
    def turn(i):
        return (4 + ((i + 1) // 2) * (2 * (i % 2) - 1)) % 8

    def to_sib(i):
        zz = (z + turn(i)) % 8
        return pltpu.make_async_remote_copy(
            part.at[zz, :, 1 - k], pbuf.at[zz], s1s.at[i], s1.at[i], device_id=sib, device_id_type=MESH
        )

    def to_pair(i):
        zz = (z + turn(i)) % 8
        return pltpu.make_async_remote_copy(
            ybuf.at[zz], yrecv.at[zz], s3s.at[i], s3.at[i], device_id=ypart, device_id_type=MESH
        )

    def to_owner(i):
        d = turn(i)
        return pltpu.make_async_remote_copy(
            sbuf.at[d], rbuf.at[d], s2s.at[d], s2.at[d], device_id=device(x, l, h, (z + d) % 8, k), device_id_type=MESH
        )

    def exchange(i):
        @pl.when(both(i >= 1, i < 9))
        def _():
            to_sib(i - 1).start()

        @pl.when(both(i >= 3, i < 11))
        def _():
            to_pair(i - 3).start()

        @pl.when(both(i >= 6, i < 13))
        def _():
            to_owner(i - 6).start()

    def chip_sum(i):
        @pl.when(both(i >= 2, i < 10))
        def _():
            zz = (z + turn(i - 2)) % 8
            arrived(pbuf.at[zz], s1.at[i - 2])
            ybuf[zz] = (part[zz, 1 - h, k] + pbuf[zz, 1 - h]).astype(BF)

        @pl.when(both(i >= 5, i < 13))
        def _():
            d = turn(i - 5)
            zz = (z + d) % 8
            arrived(yrecv.at[zz], s3.at[i - 5])
            sbuf[d] = (part[zz, h, k] + pbuf[zz, h] + yrecv[zz].astype(F32)).astype(BF)

    def span_of(i):
        return pl.ds(pl.multiple_of((z + turn(i)) % 8 * BLK, BLK), BLK)

    def values(i):
        span = span_of(i)
        points = xr[span, :]
        kern[span, :] = gaussian(points, xc[...], square_sums(points), sj[...])

    def ridge(i):
        add_ridge(kern, span_of(i), col_first - row_first - (z + turn(i)) % 8 * BLK)

    def products(i):
        part[(z + turn(i)) % 8] = dot(kern[span_of(i), :].astype(BF), coef[...]).reshape(2, 2, SHARD, NRESP)

    values(0)
    ridge(0)

    def tile_step(i, carry):
        exchange(i - 1)
        products(i - 1)
        values(i)
        ridge(i)
        chip_sum(i - 1)
        return carry

    lax.fori_loop(1, 8, tile_step, 0)
    exchange(7)
    products(7)
    chip_sum(7)

    def panel_cols(j, carry):
        span = pl.ds(pl.multiple_of(j * BLK, BLK), BLK)
        exchange(j + 8)
        p1, p2 = panels(xc[span, :], col_first + j * BLK)
        pc[span, :PANEL] = p1
        pc[span, PANEL:] = p2
        chip_sum(j + 8)
        return carry

    lax.fori_loop(0, 2, panel_cols, 0)

    def update_step(b, carry):
        exchange(b + 10)
        span = pl.ds(pl.multiple_of(b * BLK, BLK), BLK)
        kern[span, :] -= dot_t(pr[span, :], pc[...])
        chip_sum(b + 10)
        return carry

    for n in range(4):
        panel_copy(2 * n + 1 - k).wait_recv()
        panel_copy(2 * n + k).wait_send()
    lax.fori_loop(0, 8, update_step, 0)

    acc = t[...] - sbuf[0].astype(F32)
    for d in (1, 7, 2, 6, 3, 5, 4):
        arrived(rbuf.at[d], s2.at[d])
        acc = acc - rbuf[d].astype(F32)
    res[...] = acc
    for i in range(8):
        to_sib(i).wait_send()
        to_pair(i).wait_send()
        if i < 7:
            to_owner(i).wait_send()
    out.drain()


def store_kernel(kern, upd, sem):
    copies = [pltpu.make_async_copy(kern.at[pl.ds(BLK * b, BLK)], upd.at[pl.ds(BLK * b, BLK)], sem.at[b]) for b in range(8)]
    for copy in copies:
        copy.start()
    for copy in copies:
        copy.wait()


def body(descriptors, coefficients, targets, whitening):
    dma = pltpu.SemaphoreType.DMA
    vm = pl.BlockSpec(memory_space=pltpu.VMEM)
    hbm = pl.BlockSpec(memory_space=pltpu.HBM)
    V = pltpu.VMEM
    kern, residual = pl.pallas_call(
        main_kernel,
        out_shape=(
            jax.ShapeDtypeStruct((ROWS, COLS), F32),
            jax.ShapeDtypeStruct((SHARD, NRESP), F32),
        ),
        in_specs=[hbm] * 4,
        out_specs=(vm, vm),
        scratch_shapes=[
            V((ROWS, 2 * PANEL), BF), V((COLS, 2 * PANEL), BF), V((ROWS, F), BF), V((COLS, F), BF), V((8, 2, 2, 16, F), BF), V((COLS, NRESP), BF), V((2, PANEL, PANEL), F32),
            V((SHARD, NRESP), F32), V((PANEL, PANEL), BF), V((1, 2 * PANEL), F32), V((1, COLS), F32),
            V((2, PANEL, PANEL), BF), V((2, PANEL, PANEL), BF), V((BLK, 2 * PANEL), F32), V((8, 2, 2, SHARD, NRESP), F32),
            V((8, 2, SHARD, NRESP), F32), V((8, SHARD, NRESP), BF), V((8, SHARD, NRESP), BF),
            V((8, SHARD, NRESP), BF), V((8, SHARD, NRESP), BF),
            dma((180,)), dma((21,)), dma((1,)), dma((8,)), dma((8,)), dma((8,)), dma((8,)), dma((8,)), dma((8,)), dma((2,)),
            dma((2,)), dma((2,)), dma((2,)), dma((20,)), dma((1,)), dma((15,)), dma((1,)), dma((5,)),
            dma((8,)), dma((8,)), dma((8,)), dma((8,)), dma((8,)), dma((8,)), dma((4,)), dma((4,)),
        ],
        compiler_params=pltpu.CompilerParams(collective_id=0, has_side_effects=True, vmem_limit_bytes=32 << 20),
        name="main",
    )(*[pltpu.with_memory_space_constraint(a, pltpu.HBM) for a in (descriptors, coefficients, whitening, targets)])
    updated = pl.pallas_call(
        store_kernel,
        out_shape=jax.ShapeDtypeStruct((ROWS, COLS), F32),
        in_specs=[vm],
        out_specs=hbm,
        scratch_shapes=[dma((8,))],
        compiler_params=pltpu.CompilerParams(vmem_limit_bytes=16 << 20),
        name="store",
    )(kern)
    return updated, residual


def solution(mesh):
    in_specs = (P(("row", "col"), None), P("col", None), P(("row", "col"), None), P())
    out_specs = (P("row", "col"), P(("row", "col"), None))
    return jax.shard_map(body, mesh=mesh, in_specs=in_specs, out_specs=out_specs, check_vma=False)
```

time: 113 us -> 97.4 us (0.86)
  the two profiles are of different devices: /device:TPU:24 before, /device:TPU:70 now
where the time goes in v3:
time: 97.4 us; the launch traced here: 97.3 us
  Pallas kernels  96 us (99%)
    pallas_call x1, Pallas kernels, body(): pl.pallas_call(main_kernel, out_shape=(jax.ShapeDtypeStruct((ROWS, COLS),...  92.3 us
    pallas_call x1, Pallas kernels, body(): pl.pallas_call(store_kernel, out_shape=jax.ShapeDtypeStruct((ROWS, COLS),...  3.7 us

profile of v3, /device:TPU:70, one launch (start us, length us, event | category | flops | bytes accessed | tf_op | source)
XLA Modules:
  0.0 97.3 jit_solution(16939161453638750637)
XLA Ops:
  0.6 92.3 %main.1 = (f32[3072,768]{1,0:T(8,128)S(1)}, f32[96,256]{1,0:T(8,128)S(1)}) custom-call(bf16[96,768]{1,0:T(8,128)(2,1)} %x_in.1, bf16[768,256]{1,0:T(8,128)(2,1)} %coef_in.1, f32[2,256,256]{2,1,0:T(8,128)} %w_in.1, f32[96,256]{1,0:T(8,128)} %t_in.1), custom_call_target="tpu_custom_call" | custom-call | tf_op jit(solution)/shard_map/main/pallas_call | solution.py:546
  92.9 3.7 %store.1 = f32[3072,768]{1,0:T(8,128)} custom-call(f32[3072,768]{1,0:T(8,128)S(1)} %get-tuple-element.4.kern), custom_call_target="tpu_custom_call" | custom-call | tf_op jit(solution)/shard_map/store/pallas_call | solution.py:567
  96.7 0.6 copy.7

commit v4 on v3

--- a/solution.py
+++ b/solution.py
@@ -13,6 +13,7 @@
 PANEL = 256
 BLK = 384
 HALF = 48
+TAIL_BLOCKS = 2
 BF, F32 = jnp.bfloat16, jnp.float32
 SCALE = 1.4426950408889634 / (2.0 * F)
 
@@ -409,9 +410,8 @@
         panel_rows(2 * n + k)
         return carry
 
-    lax.fori_loop(0, 4, my_panels, 0)
+    lax.fori_loop(0, TAIL_BLOCKS, my_panels, 0)
     column_stage(7)
-    panel_copy(6 + k).start()
     pl.when(source)(lambda: keep.wait())
     columns_end()
 
@@ -494,22 +494,31 @@
     products(7)
     chip_sum(7)
 
+    def more_panels(n, carry):
+        exchange(n + 8 - TAIL_BLOCKS)
+        my_panels(n, carry)
+        chip_sum(n + 8 - TAIL_BLOCKS)
+        return carry
+
+    lax.fori_loop(TAIL_BLOCKS, 4, more_panels, 0)
+
     def panel_cols(j, carry):
+        pl.when(j == 1)(lambda: panel_copy(6 + k).start())
         span = pl.ds(pl.multiple_of(j * BLK, BLK), BLK)
-        exchange(j + 8)
+        exchange(j + 12 - TAIL_BLOCKS)
         p1, p2 = panels(xc[span, :], col_first + j * BLK)
         pc[span, :PANEL] = p1
         pc[span, PANEL:] = p2
-        chip_sum(j + 8)
+        chip_sum(j + 12 - TAIL_BLOCKS)
         return carry
 
     lax.fori_loop(0, 2, panel_cols, 0)
 
     def update_step(b, carry):
-        exchange(b + 10)
+        exchange(b + 14 - TAIL_BLOCKS)
         span = pl.ds(pl.multiple_of(b * BLK, BLK), BLK)
         kern[span, :] -= dot_t(pr[span, :], pc[...])
-        chip_sum(b + 10)
+        chip_sum(b + 14 - TAIL_BLOCKS)
         return carry
 
     for n in range(4):

time: 97.4 us -> 95.7 us (0.983)
  Pallas kernels: 96 us -> 94.3 us
    pallas_call x1, Pallas kernels: 92.3 us -> 90.6 us  [body(): pl.pallas_call(main_kernel, out_shape=(jax.ShapeDtypeStruct((ROWS, COLS),...]
where the time goes in v4:
time: 95.7 us; the launch traced here: 95.6 us
  Pallas kernels  94.3 us (99%)
    pallas_call x1, Pallas kernels, body(): pl.pallas_call(main_kernel, out_shape=(jax.ShapeDtypeStruct((ROWS, COLS),...  90.6 us
    pallas_call x1, Pallas kernels, body(): pl.pallas_call(store_kernel, out_shape=jax.ShapeDtypeStruct((ROWS, COLS),...  3.7 us

profile of v4, /device:TPU:70, one launch (start us, length us, event | category | flops | bytes accessed | tf_op | source)
XLA Modules:
  0.0 95.6 jit_solution(13569232390800016179)
XLA Ops:
  0.6 90.6 %main.1 = (f32[3072,768]{1,0:T(8,128)S(1)}, f32[96,256]{1,0:T(8,128)S(1)}) custom-call(bf16[96,768]{1,0:T(8,128)(2,1)} %x_in.1, bf16[768,256]{1,0:T(8,128)(2,1)} %coef_in.1, f32[2,256,256]{2,1,0:T(8,128)} %w_in.1, f32[96,256]{1,0:T(8,128)} %t_in.1), custom_call_target="tpu_custom_call" | custom-call | tf_op jit(solution)/shard_map/main/pallas_call | solution.py:555
  91.2 3.7 %store.1 = f32[3072,768]{1,0:T(8,128)} custom-call(f32[3072,768]{1,0:T(8,128)S(1)} %get-tuple-element.4.kern), custom_call_target="tpu_custom_call" | custom-call | tf_op jit(solution)/shard_map/store/pallas_call | solution.py:576
  94.9 0.6 copy.7
